TPU v7x, 32 devices: a whole 2x2x4 slice. The times are simulated.
32 devices in a mesh: seq: 4 (over z), head: 8 (over y, x, core).
Axes of the slice: x: 2, y: 2, z: 4, core: 2. Of those that a mesh axis runs over, the one named last changes fastest.
Arguments:
- inputs: bfloat16 [2048, 8192], P('seq'), may hold values from -6 to 6
- w_qkv: bfloat16 [3, 8192, 2048], P(None, None, 'head'), may hold values from -0.0625 to 0.0625
- w_out: bfloat16 [2048, 8192], P('head'), may hold values from -0.1875 to 0.1875
- turn_ids: int32 [4, 512], P('seq'), may hold values from 0 to 15, never falling along the last dimension, each value on 1 to 64 neighbouring positions
- picked: int32 [4, 64], P('seq'), may hold values from 0 to 511
- owners: int32 [256, 1], P('seq'), may hold values from 0 to 7; in each aligned block of 64 rows (0 to 63, 64 to 127, ...) at most 32 rows name the same one
- candidates: bfloat16 [2048, 8192], P(('seq', 'head')), may hold values from -0.25 to 0.25
Outputs:
- mixed: bfloat16 [2048, 8192], P('seq', 'head')
- scores: float32 [1024, 64], P(('seq', 'head'))
Inputs may be any that keep to these rules, and one draw needn't show every extreme that they name: `turn_ids`: within each session turn numbers start at 0, never fall, and each turn has 1 to 64 tokens. `owners`: among the 64 picked rows of one session no owner is named more than 32 times.
All inputs are finite; a program needn't handle non-finite values.
Results may differ from a plain program's by a relative error of at most 0.008.
Values may be sent and summed in bfloat16 or wider, within the bound.
No kernel may reach another device: no remote copies, remote signals or barrier semaphores. Data moves between devices by JAX's collectives and lax.ppermute only.
A program may use at most 128 MiB of HBM per device.

v0:
```python
import jax
import jax.numpy as jnp
from jax import lax
from jax.sharding import PartitionSpec as P

HDIM = 128


def carried_in(value, axis, join, neutral):
    count, mine = (lax.axis_size(axis), lax.axis_index(axis))
    pieces = lax.all_gather(value, axis)
    so_far = jnp.full_like(value, 0) + jnp.asarray(neutral, value.dtype)

    def lap(position, so_far):
        longer = join(so_far, pieces[position])
        return jnp.where(position < mine, longer, so_far)

    return lax.fori_loop(0, count - 1, lap, so_far)


def per_device(inputs, w_qkv, w_out, turn_ids, picked, owners, candidates):
    tokens_here = inputs.shape[0]
    model_width = inputs.shape[1]
    heads_here = w_qkv.shape[2] // HDIM
    n_head = lax.axis_size("head")
    col_count = model_width // n_head
    projected = lax.dot_general(
        inputs, w_qkv, (((1,), (1,)), ((), ())), preferred_element_type=jnp.float32
    ).astype(jnp.bfloat16)
    query = projected[:, 0].reshape(tokens_here, heads_here, HDIM)
    keys = projected[:, 1].reshape(tokens_here, heads_here, HDIM)
    values = projected[:, 2].reshape(tokens_here, heads_here, HDIM)
    states = jnp.einsum("thi,thj->hij", keys, values, preferred_element_type=jnp.float32)
    prefix = carried_in(states, "seq", jnp.add, jnp.zeros_like(states))
    prefix = prefix.astype(jnp.bfloat16)
    scores_local = jnp.einsum("thi,shi->hts", query, keys, preferred_element_type=jnp.float32)
    tok_pos = jnp.arange(tokens_here, dtype=jnp.int32)
    causal = tok_pos[:, None] >= tok_pos[None, :]
    weights = jnp.where(causal[None, :, :], scores_local, 0.0).astype(jnp.bfloat16)
    local_part = jnp.einsum("hts,shj->thj", weights, values, preferred_element_type=jnp.float32)
    carried = jnp.einsum("thi,hij->thj", query, prefix, preferred_element_type=jnp.float32)
    summed = local_part + carried
    normed = summed * lax.rsqrt(jnp.mean(summed * summed, axis=-1, keepdims=True) + 1e-05)
    attended = normed.astype(jnp.bfloat16).reshape(tokens_here, heads_here * HDIM)
    input_cols = lax.dynamic_slice_in_dim(inputs, lax.axis_index("head") * col_count, col_count, 1)
    w_cols = lax.all_to_all(w_out, "head", split_axis=1, concat_axis=0, tiled=True)
    branch = jnp.dot(
        lax.all_gather(attended, "head", axis=1, tiled=True),
        w_cols,
        preferred_element_type=jnp.float32,
    )
    mixed = (input_cols.astype(jnp.float32) + branch).astype(jnp.bfloat16)
    turn_row = turn_ids[0]
    pick_row = picked[0]
    r_dev = pick_row.shape[0]
    cap_rows = 4 * r_dev // n_head
    pick_hot = tok_pos[None, :] == pick_row[:, None]
    sel_turn = jnp.sum(jnp.where(pick_hot, turn_row[None, :], 0), axis=1)
    member = (turn_row[None, :] == sel_turn[:, None]) & (tok_pos[None, :] <= pick_row[:, None])
    row_count = jnp.sum(member.astype(jnp.float32), axis=1)
    pooled = jnp.dot(member.astype(jnp.bfloat16), mixed, preferred_element_type=jnp.float32)
    summary = (pooled / row_count[:, None]).astype(jnp.bfloat16)
    owner_row = owners[:, 0]
    row_pos = jnp.arange(r_dev, dtype=jnp.int32)
    head_pos = jnp.arange(n_head, dtype=jnp.int32)
    own_hot = (owner_row[:, None] == head_pos[None, :]).astype(jnp.int32)
    before = (row_pos[:, None] > row_pos[None, :]).astype(jnp.int32)
    slot_rank = jnp.sum(jnp.dot(before, own_hot) * own_hot, axis=1)
    slot_index = owner_row * cap_rows + slot_rank
    dispatch = (
        slot_index[None, :] == jnp.arange(n_head * cap_rows, dtype=jnp.int32)[:, None]
    ).astype(jnp.bfloat16)
    outgoing = jnp.dot(dispatch, summary, preferred_element_type=jnp.float32).astype(jnp.bfloat16)
    outgoing = outgoing.reshape(n_head, cap_rows, col_count)
    cand_parts = candidates.reshape(candidates.shape[0], n_head, col_count)
    scores = jnp.einsum(
        "skc,nsc->kn",
        lax.all_to_all(outgoing, "head", split_axis=0, concat_axis=0, tiled=True),
        cand_parts,
        preferred_element_type=jnp.float32,
    )
    return (mixed, scores)


def solution(mesh):
    return jax.shard_map(
        per_device,
        mesh=mesh,
        in_specs=(
            P("seq", None),
            P(None, None, "head"),
            P("head", None),
            P("seq", None),
            P("seq", None),
            P("seq", None),
            P(("seq", "head"), None),
        ),
        out_specs=(P("seq", "head"), P(("seq", "head"), None)),
        check_vma=False,
    )
```

profile of v0, /device:TPU:0, one launch (start us, length us, event | category | flops | bytes accessed | tf_op | source)
XLA Modules:
  0.0 109.3 jit_solution(5474585538032914516)
XLA Ops:
  7.2 6.4 %copy.43 = bf16[256,8192]{0,1:T(8,128)(2,1)} copy(bf16[256,8192]{1,0:T(8,128)(2,1)} %param.11) | data formatting | bytes 8388608 | tf_op args[2]
  13.6 5.2 %all-to-all-start = ((bf16[256,8,1024]{0,2,1:T(8,128)(2,1)}), bf16[256,8,1024]{0,2,1:T(8,128)(2,1)}, u32[]{:S(2)}, u32[]{:S(2)}) async-start(bf16[256,8,1024]{0,2,1:T(8,128)(2,1)} %bitcast.41), calls=%async_computation | async-start | bytes 8388608 | tf_op jit(solution)/shard_map/all_to_all | solution.py:46
  18.8 0.0 all-gather.3.cloned.1.call-start
  18.8 0.1 iota_compare_fusion
  18.9 12.2 %fusion.2 = bf16[512,3,256]{0,2,1:T(8,128)(2,1)S(1)} fusion(bf16[3,8192,256]{2,1,0:T(8,128)(2,1)} %param.10, bf16[512,8192]{1,0:T(8,128)(2,1)} %param.9), kind=kOutput, calls=%fused_computation.5 | convolution fusion | flops 6442844160 | bytes 21757952 | tf_op jit(solution)/shard_map/dot_general | solution.py:27
  31.1 0.1 fusion.29
  31.1 0.0 copy-start.3
  31.1 0.0 copy-start
  31.2 0.0 copy-start.1
  31.2 0.2 fusion.30
  31.4 17.1 %all-gather = f32[8,128,128]{2,1,0:T(8,128)S(1)} all-gather(f32[2,128,128]{2,1,0:T(8,128)S(1)} %fusion.30), channel_id=2, replica_groups=mesh['seq'=4,'head'=8] {'seq'}, dimensions={0}, use_global_device_ids=true | all-gather | bytes 655360 | tf_op jit(solution)/shard_map/all_gather | solution.py:11
  48.5 0.2 while.14
  48.7 0.3 fusion.23
  49.0 0.8 multiply_reduce_fusion
  49.8 0.7 multiply_convert_fusion
  50.5 0.0 all-gather.3.cloned.1.call-update
  50.6 0.0 copy-done.3
  50.6 0.1 fusion.9
  50.7 0.0 copy-done
  50.7 0.0 copy-done.1
  50.7 0.2 select_reduce_fusion
  50.9 0.2 convert_reduce_fusion
  51.1 19.6 %all-to-all-done = bf16[256,8,1024]{0,2,1:T(8,128)(2,1)} async-done(((bf16[256,8,1024]{0,2,1:T(8,128)(2,1)}), bf16[256,8,1024]{0,2,1:T(8,128)(2,1)}, u32[]{:S(2)}, u32[]{:S(2)}) %all-to-all-start) | async-done | bytes 4194336 | tf_op jit(solution)/shard_map/all_to_all | solution.py:46
  70.8 6.5 %copy.44 = bf16[8,256,1024]{2,1,0:T(8,128)(2,1)} copy(bf16[8,256,1024]{1,2,0:T(8,128)(2,1)} %bitcast.8) | data formatting | bytes 8388608 | tf_op jit(solution)/shard_map/all_to_all | solution.py:46
  77.2 5.9 %all-gather.3.cloned.1.call-done = bf16[512,2048]{0,1:T(8,128)(2,1)} async-done(((bf16[512,256]{0,1:T(8,128)(2,1)}), bf16[512,2048]{0,1:T(8,128)(2,1)}) %all-gather.3.cloned.1.call-update) | async-done | bytes 2097168 | tf_op jit(solution)/shard_map/all_gather | solution.py:48
  83.1 0.0 copy-start.2
  83.1 5.5 %add_convert_fusion = bf16[512,1024]{1,0:T(8,128)(2,1)S(1)} fusion(bf16[512,2048]{0,1:T(8,128)(2,1)} %all-gather.3.cloned.1.call-done, bf16[2048,1024]{1,0:T(8,128)(2,1)} %bitcast.42, bf16[512,8192]{1,0:T(8,128)(2,1)} %param.9, s32[]{:T(128)S(6)} %select_n.32), kind=kOutput, calls=%fused_computation.3 | convolution fusion | flops 2149056512 | bytes 8388612 | tf_op jit(solution)/shard_map/dot_general | solution.py:47
  88.6 0.0 copy-start.4
  88.6 0.5 convolution_convert_fusion
  89.2 12.3 %all_to_all.24 = bf16[8,32,1024]{2,1,0:T(8,128)(2,1)S(1)} all-to-all(bf16[8,32,1024]{2,1,0:T(8,128)(2,1)S(1)} %bitcast.51), channel_id=1, replica_groups=mesh['seq'=4,'head'=8] {'head'}, dimensions={0} | all-to-all | bytes 1048576 | tf_op jit(solution)/shard_map/all_to_all | solution.py:78
  101.4 0.0 copy-done.2
  101.4 1.0 convolution_bitcast_fusion
  102.5 0.0 copy-done.4
  (6 shorter events, 0.1 us)
Async XLA Ops:
  13.6 57.2 %all-to-all-start = ((bf16[256,8,1024]{0,2,1:T(8,128)(2,1)}), bf16[256,8,1024]{0,2,1:T(8,128)(2,1)}, u32[]{:S(2)}, u32[]{:S(2)}) async-start(bf16[256,8,1024]{0,2,1:T(8,128)(2,1)} %bitcast.41), calls=%async_computation | async-start | bytes 8388608 | tf_op jit(solution)/shard_map/all_to_all | solution.py:46
  18.8 64.3 %all-gather.3.cloned.1.call-start = ((), (), s32[]{:S(2)}) async-start(), calls=%async_computation.2 | async-start | bytes 2359296 | tf_op jit(solution)/shard_map/all_gather | solution.py:48
  31.1 19.4 %copy-start.3 = (s32[64,1]{0,1:T(1,128)S(1)}, s32[64,1]{0,1:T(1,128)}, u32[]{:S(2)}) copy-start(s32[64,1]{0,1:T(1,128)} %param.14) | copy-start | bytes 772
  31.1 19.6 %copy-start = (s32[1,512]{1,0:T(1,128)S(1)}, s32[1,512]{1,0:T(1,128)}, u32[]{:S(2)}) copy-start(s32[1,512]{1,0:T(1,128)} %param.12) | copy-start | bytes 6148
  31.2 19.6 %copy-start.1 = (s32[1,64]{1,0:T(1,128)S(1)}, s32[1,64]{1,0:T(1,128)}, u32[]{:S(2)}) copy-start(s32[1,64]{1,0:T(1,128)} %param.13) | copy-start | bytes 772
  83.1 18.3 %copy-start.2 = (bf16[64,8192]{1,0:T(8,128)(2,1)S(1)}, bf16[64,8192]{1,0:T(8,128)(2,1)}, u32[]{:S(2)}) copy-start(bf16[64,8192]{1,0:T(8,128)(2,1)} %param.15) | copy-start | bytes 3145732
  88.6 13.8 %copy-start.4 = (bf16[512,1024]{1,0:T(8,128)(2,1)}, bf16[512,1024]{1,0:T(8,128)(2,1)S(1)}, u32[]{:S(2)}) copy-start(bf16[512,1024]{1,0:T(8,128)(2,1)S(1)} %add_convert_fusion) | copy-start | bytes 3145732
Sparse Core Ops, SparseCore 0:
  50.7 32.3 all-gather.2
where the time goes:
time: 110 us; the launch traced here: 109 us
  blocking collectives  29.4 us (27%)
  waiting for transfers between devices  25.5 us (23%)
  matrix products  20.7 us (19%)
  between operations  14.2 us (13%)
  local copies, waits for them, and re-layouts  13 us (12%)
  starting transfers between devices  5.23 us (5%)
  other arithmetic  1.34 us (1%)
    all_to_all x1, waiting for transfers between devices, per_device(): lax.all_to_all(w_out, 'head', split_axis=1, concat_axis=0, tiled=True)  19.6 us
    all_gather x1, blocking collectives, carried_in(): pieces = lax.all_gather(value, axis)  17.1 us
    all_to_all x1, blocking collectives, per_device(): lax.all_to_all(outgoing, 'head', split_axis=0, concat_axis=0, tiled=True)  12.3 us
    dot_general x1, matrix products, per_device(): lax.dot_general(inputs, w_qkv, (((1,), (1,)), ((), ())), preferred_elemen...  12.2 us
    all_to_all x1, local copies, waits for them, and re-layouts, per_device(): lax.all_to_all(w_out, 'head', split_axis=1, concat_axis=0, tiled=True)  6.48 us
    unnamed x11, local copies, waits for them, and re-layouts  6.43 us
    all_gather x1, waiting for transfers between devices, per_device(): lax.all_gather(attended, 'head', axis=1, tiled=True)  5.86 us
    dot_general x1, matrix products, per_device(): jnp.dot(lax.all_gather(attended, 'head', axis=1, tiled=True), w_cols, pre...  5.52 us
  transfers between devices with their start and end apart: 2, of which 2 were waited for; matrix products, arithmetic and copies ran while one was open for 20% of the time, Pallas kernels for 0%

commit v1 on v0

--- a/solution.py
+++ b/solution.py
@@ -44,11 +44,16 @@
     attended = normed.astype(jnp.bfloat16).reshape(tokens_here, heads_here * HDIM)
     input_cols = lax.dynamic_slice_in_dim(inputs, lax.axis_index("head") * col_count, col_count, 1)
     w_cols = lax.all_to_all(w_out, "head", split_axis=1, concat_axis=0, tiled=True)
-    branch = jnp.dot(
-        lax.all_gather(attended, "head", axis=1, tiled=True),
-        w_cols,
-        preferred_element_type=jnp.float32,
+    solve_face = lambda my_data, pos_dim: jnp.concatenate(
+        lax.all_to_all(
+            jnp.stack(lax.psum(1, axis_name="head") * [my_data], 0),
+            axis_name="head",
+            split_axis=0,
+            concat_axis=0,
+        ),
+        pos_dim,
     )
+    branch = jnp.dot(solve_face(attended, pos_dim=1), w_cols, preferred_element_type=jnp.float32)
     mixed = (input_cols.astype(jnp.float32) + branch).astype(jnp.bfloat16)
     turn_row = turn_ids[0]
     pick_row = picked[0]

time: 110 us -> 139 us (1.26)
  waiting for transfers between devices: 25.5 us -> 62.3 us
  between operations: 14.2 us -> 0.79 us
  starting transfers between devices: 5.23 us -> 8.27 us
  matrix products: 20.7 us -> 22.3 us
  local copies, waits for them, and re-layouts: 13 us -> 14.6 us
    all_to_all x1, waiting for transfers between devices: 19.6 us -> 48.5 us  [per_device(): lax.all_to_all(w_out, 'head', split_axis=1, concat_axis=0, tiled=True)]
    all_to_all x0 -> x1, waiting for transfers between devices: none -> 13.8 us  [per_device(): lax.all_to_all(jnp.stack(lax.psum(1, axis_name='head') * [my_data], 0), a...]
    all_gather x1 -> x0, waiting for transfers between devices: 5.86 us -> none  [per_device(): lax.all_gather(attended, 'head', axis=1, tiled=True)]
    all_to_all x0 -> x1, starting transfers between devices: none -> 3.72 us  [per_device(): lax.all_to_all(jnp.stack(lax.psum(1, axis_name='head') * [my_data], 0), a...]
    another operation x0 -> x2, local copies, waits for them, and re-layouts: none -> 1.66 us  [per_device(): jnp.stack(lax.psum(1, axis_name='head') * [my_data], 0)]
    unnamed x11 -> x9, local copies, waits for them, and re-layouts: 6.43 us -> 6.4 us
  transfers between devices with their start and end apart: 2 -> 2, of which waited for: 2 -> 2; matrix products, arithmetic and copies ran while one was open for 20% -> 10% of each run, Pallas kernels for 0% -> 0%
where the time goes in v1:
time: 139 us; the launch traced here: 138 us
  waiting for transfers between devices  62.3 us (45%)
  blocking collectives  29.5 us (21%)
  matrix products  22.3 us (16%)
  local copies, waits for them, and re-layouts  14.6 us (11%)
  starting transfers between devices  8.27 us (6%)
    all_to_all x1, waiting for transfers between devices, per_device(): lax.all_to_all(w_out, 'head', split_axis=1, concat_axis=0, tiled=True)  48.5 us
    all_gather x1, blocking collectives, carried_in(): pieces = lax.all_gather(value, axis)  17.4 us
    all_to_all x1, waiting for transfers between devices, per_device(): lax.all_to_all(jnp.stack(lax.psum(1, axis_name='head') * [my_data], 0), a...  13.8 us
    dot_general x1, matrix products, per_device(): lax.dot_general(inputs, w_qkv, (((1,), (1,)), ((), ())), preferred_elemen...  12.3 us
    all_to_all x1, blocking collectives, per_device(): lax.all_to_all(outgoing, 'head', split_axis=0, concat_axis=0, tiled=True)  12.1 us
    all_to_all x1, local copies, waits for them, and re-layouts, per_device(): lax.all_to_all(w_out, 'head', split_axis=1, concat_axis=0, tiled=True)  6.44 us
    unnamed x9, local copies, waits for them, and re-layouts  6.4 us
    dot_general x1, matrix products, per_device(): jnp.dot(solve_face(attended, pos_dim=1), w_cols, preferred_element_type=j...  5.79 us
  transfers between devices with their start and end apart: 2, of which 2 were waited for; matrix products, arithmetic and copies ran while one was open for 10% of the time, Pallas kernels for 0%

profile of v1, /device:TPU:0, one launch (start us, length us, event | category | flops | bytes accessed | tf_op | source)
XLA Modules:
  0.0 138.4 jit_solution(213632650046916514)
XLA Ops:
  0.6 0.1 iota_compare_fusion
  0.7 12.3 %fusion.6 = bf16[512,3,256]{0,2,1:T(8,128)(2,1)S(1)} fusion(bf16[3,8192,256]{2,1,0:T(8,128)(2,1)} %param.10, bf16[512,8192]{1,0:T(8,128)(2,1)} %param.9), kind=kOutput, calls=%fused_computation.9 | convolution fusion | flops 6442844160 | bytes 21757952 | tf_op jit(solution)/shard_map/dot_general | solution.py:27
  13.0 0.1 fusion.37
  13.1 0.2 fusion.38
  13.3 17.4 %all-gather = f32[8,128,128]{2,1,0:T(8,128)S(1)} all-gather(f32[2,128,128]{2,1,0:T(8,128)S(1)} %fusion.38), channel_id=2, replica_groups=mesh['seq'=4,'head'=8] {'seq'}, dimensions={0}, use_global_device_ids=true | all-gather | bytes 655360 | tf_op jit(solution)/shard_map/all_gather | solution.py:11
  30.7 0.2 while.14
  30.9 0.3 fusion.31
  31.1 0.8 multiply_reduce_fusion
  32.0 0.1 copy.39
  32.2 1.5 %stack.3 = bf16[8,512,256]{2,1,0:T(8,128)(2,1)} broadcast(bf16[512,256]{1,0:T(8,128)(2,1)S(1)} %copy.39), dimensions={1,2} | broadcast | bytes 2359296 | tf_op jit(solution)/shard_map/stack | solution.py:49
  33.7 3.7 %all-to-all-start = ((bf16[8,512,256]{2,1,0:T(8,128)(2,1)}), bf16[8,512,256]{2,1,0:T(8,128)(2,1)S(1)}, u32[]{:S(2)}, u32[]{:S(2)}) async-start(bf16[8,512,256]{2,1,0:T(8,128)(2,1)} %stack.3), calls=%async_computation | async-start | bytes 4194304 | tf_op jit(solution)/shard_map/all_to_all | solution.py:48
  37.4 6.4 %copy.40 = bf16[256,8192]{0,1:T(8,128)(2,1)} copy(bf16[256,8192]{1,0:T(8,128)(2,1)} %param.11) | data formatting | bytes 8388608 | tf_op args[2]
  43.8 6.4 %copy.41 = bf16[256,8,1024]{2,0,1:T(8,128)(2,1)} copy(bf16[256,8,1024]{0,2,1:T(8,128)(2,1)} %bitcast.51) | data formatting | bytes 8388608 | tf_op jit(solution)/shard_map/all_to_all | solution.py:46
  50.2 0.0 copy-start.3
  50.2 0.0 copy-start
  50.2 0.0 copy-start.1
  50.2 13.8 %all-to-all-done = bf16[8,512,256]{2,1,0:T(8,128)(2,1)S(1)} async-done(((bf16[8,512,256]{2,1,0:T(8,128)(2,1)}), bf16[8,512,256]{2,1,0:T(8,128)(2,1)S(1)}, u32[]{:S(2)}, u32[]{:S(2)}) %all-to-all-start) | async-done | bytes 2097184 | tf_op jit(solution)/shard_map/all_to_all | solution.py:48
  64.0 4.5 %all-to-all-start.1 = ((bf16[256,8,1024]{2,0,1:T(8,128)(2,1)}), bf16[256,8,1024]{2,0,1:T(8,128)(2,1)}, u32[]{:S(2)}, u32[]{:S(2)}) async-start(bf16[256,8,1024]{2,0,1:T(8,128)(2,1)} %copy.41), calls=%async_computation.1 | async-start | bytes 8388608 | tf_op jit(solution)/shard_map/all_to_all | solution.py:46
  68.6 0.0 copy-done.3
  68.6 0.1 fusion.17
  68.7 0.0 copy-done
  68.7 0.0 copy-done.1
  68.8 0.2 select_reduce_fusion
  68.9 0.2 convert_reduce_fusion
  69.1 0.0 copy-start.2
  69.2 48.5 %all-to-all-done.1 = bf16[256,8,1024]{2,0,1:T(8,128)(2,1)} async-done(((bf16[256,8,1024]{2,0,1:T(8,128)(2,1)}), bf16[256,8,1024]{2,0,1:T(8,128)(2,1)}, u32[]{:S(2)}, u32[]{:S(2)}) %all-to-all-start.1) | async-done | bytes 4194336 | tf_op jit(solution)/shard_map/all_to_all | solution.py:46
  117.7 5.8 %fusion.4 = bf16[512,1024]{1,0:T(8,128)(2,1)} fusion(bf16[256,8,1024]{2,0,1:T(8,128)(2,1)} %all-to-all-done.1, bf16[8,512,256]{2,1,0:T(8,128)(2,1)S(1)} %all-to-all-done, bf16[512,8192]{1,0:T(8,128)(2,1)} %param.9, s32[]{:T(128)S(6)} %select_n.32), kind=kOutput, calls=%fused_computation.6 | convolution fusion | flops 2149056512 | bytes 8388612 | tf_op jit(solution)/shard_map/dot_general | solution.py:56
  123.5 1.8 %convolution_convert_fusion = bf16[256,1024]{1,0:T(8,128)(2,1)S(1)} fusion(bf16[512,1024]{1,0:T(8,128)(2,1)} %fusion.4, f32[64]{0:T(128)S(1)} %convert_reduce_fusion, s32[64]{0:T(128)S(1)} %bitcast.66, s32[512]{0:T(512)S(1)} %bitcast.63, s32[64]{0:T(128)S(1)} %multiply_add_fusion, s32[64]{0:T(128)S(1)} %select_reduce_fusion), kind=kOutput, calls=%fused_computation.11 | convolution fusion | flops 101171200 | bytes 1575936 | tf_op jit(solution)/shard_map/dot_general | solution.py:78
  125.2 12.1 %all_to_all.26 = bf16[8,32,1024]{2,1,0:T(8,128)(2,1)S(1)} all-to-all(bf16[8,32,1024]{2,1,0:T(8,128)(2,1)S(1)} %bitcast.60), channel_id=1, replica_groups=mesh['seq'=4,'head'=8] {'head'}, dimensions={0} | all-to-all | bytes 1048576 | tf_op jit(solution)/shard_map/all_to_all | solution.py:83
  137.4 0.0 copy-done.2
  137.4 1.0 convolution_bitcast_fusion
  (7 shorter events, 0.2 us)
Async XLA Ops:
  33.7 30.3 %all-to-all-start = ((bf16[8,512,256]{2,1,0:T(8,128)(2,1)}), bf16[8,512,256]{2,1,0:T(8,128)(2,1)S(1)}, u32[]{:S(2)}, u32[]{:S(2)}) async-start(bf16[8,512,256]{2,1,0:T(8,128)(2,1)} %stack.3), calls=%async_computation | async-start | bytes 4194304 | tf_op jit(solution)/shard_map/all_to_all | solution.py:48
  50.2 18.4 %copy-start.3 = (s32[64,1]{0,1:T(1,128)S(1)}, s32[64,1]{0,1:T(1,128)}, u32[]{:S(2)}) copy-start(s32[64,1]{0,1:T(1,128)} %param.14) | copy-start | bytes 772
  50.2 18.5 %copy-start = (s32[1,512]{1,0:T(1,128)S(1)}, s32[1,512]{1,0:T(1,128)}, u32[]{:S(2)}) copy-start(s32[1,512]{1,0:T(1,128)} %param.12) | copy-start | bytes 6148
  50.2 18.5 %copy-start.1 = (s32[1,64]{1,0:T(1,128)S(1)}, s32[1,64]{1,0:T(1,128)}, u32[]{:S(2)}) copy-start(s32[1,64]{1,0:T(1,128)} %param.13) | copy-start | bytes 772
  64.0 53.7 %all-to-all-start.1 = ((bf16[256,8,1024]{2,0,1:T(8,128)(2,1)}), bf16[256,8,1024]{2,0,1:T(8,128)(2,1)}, u32[]{:S(2)}, u32[]{:S(2)}) async-start(bf16[256,8,1024]{2,0,1:T(8,128)(2,1)} %copy.41), calls=%async_computation.1 | async-start | bytes 8388608 | tf_op jit(solution)/shard_map/all_to_all | solution.py:46
  69.1 68.2 %copy-start.2 = (bf16[64,8192]{1,0:T(8,128)(2,1)S(1)}, bf16[64,8192]{1,0:T(8,128)(2,1)}, u32[]{:S(2)}) copy-start(bf16[64,8192]{1,0:T(8,128)(2,1)} %param.15) | copy-start | bytes 3145732
